TPU v7x, 256 devices: a whole 4x4x8 slice. The times are simulated.
256 devices in a mesh: gal: 8 (over y, core), pix: 32 (over x, z).
Axes of the slice: x: 4, y: 4, z: 8, core: 2. Of those that a mesh axis runs over, the one named last changes fastest.
Arguments:
- observed: float32 [32768, 4096], P('pix', 'gal'), may hold values from -6 to 6
- sparse_init: float32 [32768, 4096], P('pix', 'gal'), may hold values from -4 to 4
- dual_init: float32 [32768, 4096], P('pix', 'gal'), may hold values from -4 to 4
- right_init: float32 [64, 4096], P(None, 'gal'), may hold values from -0.09375 to 0.09375
Outputs:
- sparse: float32 [32768, 4096], P('pix', 'gal')
- dual: float32 [32768, 4096], P('pix', 'gal')
- left: float32 [64, 32768], P(None, 'pix')
- right: float32 [64, 4096], P(None, 'gal')
All inputs are finite; a program needn't handle non-finite values.
Results may differ from a plain program's by a relative error of at most 0.0003.
Values sent between devices are 32-bit elements; how exact they have to be, the bound alone decides.
A program may use at most 64 MiB of HBM per device.

v0:
```python
import jax
import jax.numpy as jnp
from jax import lax
from jax.sharding import PartitionSpec as P

ITERS = 2
MU = 1.25
TAU = 0.6 / 1.25
HIGH = lax.Precision.HIGHEST


def gram_of(panel):
    return lax.dot_general(panel, panel, (((1,), (1,)), ((), ())), precision=HIGH)


def orth_with(panel, gram):
    factor = jnp.linalg.cholesky(gram)
    return jax.scipy.linalg.solve_triangular(factor, panel, lower=True)


def shrink(values):
    return jnp.sign(values) * jnp.maximum(jnp.abs(values) - TAU, 0.0)


def per_device(observed, sparse_init, dual_init, right_init):
    sparse, dual, right = (sparse_init, dual_init, right_init)
    left = None
    for step in range(ITERS):
        target = observed - sparse + dual / MU
        partial_left = lax.dot_general(right, target, (((1,), (1,)), ((), ())), precision=HIGH)
        panel = lax.psum(partial_left, "gal")
        gram_left = lax.psum(gram_of(panel), "pix")
        left = orth_with(panel, gram_left)
        partial_wide = jnp.dot(left, target, precision=HIGH)
        wide = lax.psum(partial_wide, "pix")
        lowrank = lax.dot_general(left, wide, (((0,), (0,)), ((), ())), precision=HIGH)
        sparse = shrink(observed - lowrank + dual / MU)
        dual = dual + MU * (observed - lowrank - sparse)
        gram_right = lax.psum(gram_of(wide), "gal")
        right = orth_with(wide, gram_right)
    return (sparse, dual, left, right)


def solution(mesh):
    return jax.shard_map(
        per_device,
        mesh=mesh,
        in_specs=(P("pix", "gal"), P("pix", "gal"), P("pix", "gal"), P(None, "gal")),
        out_specs=(P("pix", "gal"), P("pix", "gal"), P(None, "pix"), P(None, "gal")),
        check_vma=False,
    )
```

profile of v0, /device:TPU:2, one launch (start us, length us, event | category | flops | bytes accessed | tf_op | source)
XLA Modules:
  0.0 836.8 jit_solution(9455242366928281128)
XLA Ops:
  7.2 0.8 copy-done
  8.1 6.0 convolution_bitcast_fusion
  14.2 68.6 %all-reduce.5.cloned.1.call-done = f32[64,1024]{1,0:T(8,128)} async-done(((f32[64,1024]{1,0:T(8,128)}), f32[64,1024]{1,0:T(8,128)}) %all-reduce.5.cloned.1.call-update) | async-done | bytes 262160 | tf_op jit(solution)/shard_map/psum | solution.py:31
  82.7 1.4 fusion.21
  84.1 131.0 %psum.57 = f32[64,64]{0,1:T(8,128)S(1)} all-reduce(f32[64,64]{0,1:T(8,128)S(1)} %fusion.21), channel_id=1, replica_groups=mesh['gal'=8,'pix'=32] {'pix'}, use_global_device_ids=true, to_apply=%region_1.0 | all-reduce | flops 4096 | bytes 32768 | tf_op jit(solution)/shard_map/psum | solution.py:32
  215.3 5.8 cholesky.74
  221.8 0.7 fusion
  222.5 4.9 custom-call.10
  227.4 1.4 fusion.13
  228.7 4.4 fusion.20
  233.3 145.8 %all-reduce.7.cloned.1.call-done = f32[64,512]{1,0:T(8,128)} async-done(((f32[64,512]{1,0:T(8,128)}), f32[64,512]{1,0:T(8,128)}) %all-reduce.7.cloned.1.call-update) | async-done | bytes 131088 | tf_op jit(solution)/shard_map/psum | solution.py:35
  379.0 1.2 fusion.22
  380.3 23.8 %psum.59 = f32[64,64]{0,1:T(8,128)S(1)} all-reduce(f32[64,64]{0,1:T(8,128)S(1)} %fusion.22), channel_id=1, replica_groups=mesh['gal'=8,'pix'=32] {'gal'}, use_global_device_ids=true, to_apply=%region_5.8 | all-reduce | flops 4096 | bytes 32768 | tf_op jit(solution)/shard_map/psum | solution.py:39
  404.2 5.8 cholesky.85
  411.4 4.9 custom-call.11
  416.3 6.1 subtract_add_fusion
  422.7 1.0 copy-done.2
  423.7 2.8 fusion.23
  426.6 61.5 %all-reduce.9.cloned.1.call-done = f32[64,1024]{1,0:T(8,128)} async-done(((f32[64,1024]{1,0:T(8,128)}), f32[64,1024]{1,0:T(8,128)}) %all-reduce.9.cloned.1.call-update) | async-done | bytes 262160 | tf_op jit(solution)/shard_map/psum | solution.py:31
  488.1 1.4 fusion.24
  489.5 131.0 %psum.61 = f32[64,64]{0,1:T(8,128)S(1)} all-reduce(f32[64,64]{0,1:T(8,128)S(1)} %fusion.24), channel_id=1, replica_groups=mesh['gal'=8,'pix'=32] {'pix'}, use_global_device_ids=true, to_apply=%region_7.0 | all-reduce | flops 4096 | bytes 32768 | tf_op jit(solution)/shard_map/psum | solution.py:32
  620.7 5.8 cholesky.96
  627.8 4.9 custom-call.12
  632.7 1.4 fusion.7
  634.1 3.7 fusion.25
  637.9 145.9 %all-reduce.11.cloned.1.call-done = f32[64,512]{1,0:T(8,128)} async-done(((f32[64,512]{1,0:T(8,128)}), f32[64,512]{1,0:T(8,128)}) %all-reduce.11.cloned.1.call-update) | async-done | bytes 131088 | tf_op jit(solution)/shard_map/psum | solution.py:35
  783.7 1.2 fusion.26
  785.0 23.8 %psum.63 = f32[64,64]{0,1:T(8,128)S(1)} all-reduce(f32[64,64]{0,1:T(8,128)S(1)} %fusion.26), channel_id=1, replica_groups=mesh['gal'=8,'pix'=32] {'gal'}, use_global_device_ids=true, to_apply=%region_9.13 | all-reduce | flops 4096 | bytes 32768 | tf_op jit(solution)/shard_map/psum | solution.py:39
  808.9 5.8 cholesky.107
  816.1 4.9 custom-call.13
  821.0 8.2 multiply_add_fusion
  829.3 1.0 fusion.4
  (38 shorter events, 5.6 us)
Async XLA Ops:
  7.2 0.9 copy-start
  7.2 75.6 %all-reduce.5.cloned.1.call-start = ((), (), s32[]{:S(2)}) async-start(), calls=%async_computation | async-start | bytes 524288 | tf_op jit(solution)/shard_map/psum | solution.py:31
  8.1 220.7 %copy-start.1 = (f32[1024,512]{1,0:T(8,128)S(1)}, f32[1024,512]{1,0:T(8,128)}, u32[]{:S(2)}) copy-start(f32[1024,512]{1,0:T(8,128)} %param.11) | copy-start | bytes 6291460
  14.1 364.9 %all-reduce.7.cloned.1.call-start = ((), (), s32[]{:S(2)}) async-start(), calls=%async_computation.1 | async-start | bytes 262144 | tf_op jit(solution)/shard_map/psum | solution.py:35
  233.2 254.9 %all-reduce.9.cloned.1.call-start = ((), (), s32[]{:S(2)}) async-start(), calls=%async_computation.2 | async-start | bytes 524288 | tf_op jit(solution)/shard_map/psum | solution.py:31
  416.2 6.2 copy-start.4
  422.4 1.3 copy-start.2
  426.6 357.1 %all-reduce.11.cloned.1.call-start = ((), (), s32[]{:S(2)}) async-start(), calls=%async_computation.3 | async-start | bytes 262144 | tf_op jit(solution)/shard_map/psum | solution.py:35
  634.1 195.1 %copy-start.3 = (f32[64,1024]{1,0:T(8,128)}, f32[64,1024]{1,0:T(8,128)S(1)}, u32[]{:S(2)}) copy-start(f32[64,1024]{1,0:T(8,128)S(1)} %fusion.7) | copy-start | bytes 786436
  821.0 8.3 copy-start.5
Sparse Core Ops, SparseCore 0:
  14.3 68.4 all-reduce.4
  233.3 145.6 all-reduce.6
  426.7 61.3 all-reduce.8
  638.0 145.6 all-reduce.10
where the time goes:
time: 837 us
  waiting for transfers between devices  422 us (50%)
  blocking collectives  310 us (37%)
  other arithmetic  48.3 us (6%)
  matrix products  40.7 us (5%)
  between operations  14 us (2%)
    psum x2, waiting for transfers between devices, per_device(): wide = lax.psum(partial_wide, 'pix')  292 us
    psum x2, blocking collectives, per_device(): gram_left = lax.psum(gram_of(panel), 'pix')  262 us
    psum x2, waiting for transfers between devices, per_device(): panel = lax.psum(partial_left, 'gal')  130 us
    psum x2, blocking collectives, per_device(): gram_right = lax.psum(gram_of(wide), 'gal')  47.6 us
    another operation x12, other arithmetic, orth_with(): factor = jnp.linalg.cholesky(gram)  26.1 us
    another operation x8, other arithmetic, orth_with(): return jax.scipy.linalg.solve_triangular(factor, panel, lower=True)  22.2 us
  transfers between devices with their start and end apart: 4, of which 4 were waited for; matrix products, arithmetic and copies ran while one was open for 0% of the time, Pallas kernels for 0%

commit v1 on v0

--- a/solution.py
+++ b/solution.py
@@ -28,7 +28,9 @@
     for step in range(ITERS):
         target = observed - sparse + dual / MU
         partial_left = lax.dot_general(right, target, (((1,), (1,)), ((), ())), precision=HIGH)
-        panel = lax.psum(partial_left, "gal")
+        panel = partial_left
+        for hop in (1, 2, 4):
+            panel = panel + lax.ppermute(panel, "gal", [(dev, dev ^ hop) for dev in range(8)])
         gram_left = lax.psum(gram_of(panel), "pix")
         left = orth_with(panel, gram_left)
         partial_wide = jnp.dot(left, target, precision=HIGH)

time: 837 us -> 742 us (0.89)
  waiting for transfers between devices: 422 us -> 327 us
    psum x2 -> x0, waiting for transfers between devices: 130 us -> none  [per_device(): panel = lax.psum(partial_left, 'gal')]
    ppermute x0 -> x6, waiting for transfers between devices: none -> 32.9 us  [per_device(): lax.ppermute(panel, 'gal', [(dev, dev ^ hop) for dev in range(8)])]
  transfers between devices with their start and end apart: 4 -> 8, of which waited for: 4 -> 8; matrix products, arithmetic and copies ran while one was open for 0% -> 0% of each run, Pallas kernels for 0% -> 0%
where the time goes in v1:
time: 742 us
  waiting for transfers between devices  327 us (44%)
  blocking collectives  310 us (42%)
  other arithmetic  48.5 us (7%)
  matrix products  35.2 us (5%)
  between operations  14.3 us (2%)
    psum x2, waiting for transfers between devices, per_device(): wide = lax.psum(partial_wide, 'pix')  295 us
    psum x2, blocking collectives, per_device(): gram_left = lax.psum(gram_of(panel), 'pix')  263 us
    psum x2, blocking collectives, per_device(): gram_right = lax.psum(gram_of(wide), 'gal')  47.4 us
    ppermute x6, waiting for transfers between devices, per_device(): lax.ppermute(panel, 'gal', [(dev, dev ^ hop) for dev in range(8)])  32.9 us
    another operation x12, other arithmetic, orth_with(): factor = jnp.linalg.cholesky(gram)  26.1 us
    another operation x8, other arithmetic, orth_with(): return jax.scipy.linalg.solve_triangular(factor, panel, lower=True)  22.2 us
  transfers between devices with their start and end apart: 8, of which 8 were waited for; matrix products, arithmetic and copies ran while one was open for 0% of the time, Pallas kernels for 0%

profile of v1, /device:TPU:2, one launch (start us, length us, event | category | flops | bytes accessed | tf_op | source)
XLA Modules:
  0.0 742.1 jit_solution(4524972640222490992)
XLA Ops:
  7.2 0.8 copy-done
  8.1 5.2 convolution_bitcast_fusion
  13.4 1.5 collective-permute-done
  14.9 1.7 collective-permute-start.1
  16.6 6.8 collective-permute-done.1
  23.4 3.3 collective-permute-start.2
  26.7 5.8 collective-permute-done.2
  32.9 133.6 %psum.42 = f32[64,64]{0,1:T(8,128)S(1)} all-reduce(f32[64,64]{0,1:T(8,128)S(1)} %fusion.21), channel_id=1, replica_groups=mesh['gal'=8,'pix'=32] {'pix'}, use_global_device_ids=true, to_apply=%region_0.0 | all-reduce | flops 4096 | bytes 32768 | tf_op jit(solution)/shard_map/psum | solution.py:34
  166.6 5.8 cholesky.74
  173.8 4.9 custom-call.10
  179.1 4.4 fusion.20
  183.6 148.5 %all-reduce.3.cloned.1.call-done = f32[64,512]{1,0:T(8,128)} async-done(((f32[64,512]{1,0:T(8,128)}), f32[64,512]{1,0:T(8,128)}) %all-reduce.3.cloned.1.call-update) | async-done | bytes 131088 | tf_op jit(solution)/shard_map/psum | solution.py:37
  332.1 1.2 fusion.22
  333.4 23.8 %psum.44 = f32[64,64]{0,1:T(8,128)S(1)} all-reduce(f32[64,64]{0,1:T(8,128)S(1)} %fusion.22), channel_id=1, replica_groups=mesh['gal'=8,'pix'=32] {'gal'}, use_global_device_ids=true, to_apply=%region_4.7 | all-reduce | flops 4096 | bytes 32768 | tf_op jit(solution)/shard_map/psum | solution.py:41
  357.3 5.8 cholesky.85
  364.4 4.9 custom-call.11
  369.4 6.1 subtract_add_fusion
  375.8 2.1 fusion.23
  378.1 1.5 collective-permute-done.3
  379.7 8.3 %collective-permute-done.4 = f32[64,1024]{1,0:T(8,128)S(1)} collective-permute-done((f32[64,1024]{1,0:T(8,128)S(1)}, f32[64,1024]{1,0:T(8,128)S(1)}, u32[]{:S(2)}, u32[]{:S(2)}) %collective-permute-start.4) | collective-permute-done | bytes 262176 | tf_op jit(solution)/shard_map/ppermute | solution.py:33
  388.2 9.0 %collective-permute-done.5 = f32[64,1024]{1,0:T(8,128)S(1)} collective-permute-done((f32[64,1024]{1,0:T(8,128)S(1)}, f32[64,1024]{1,0:T(8,128)S(1)}, u32[]{:S(2)}, u32[]{:S(2)}) %collective-permute-start.5) | collective-permute-done | bytes 262176 | tf_op jit(solution)/shard_map/ppermute | solution.py:33
  397.6 129.1 %psum.45 = f32[64,64]{0,1:T(8,128)S(1)} all-reduce(f32[64,64]{0,1:T(8,128)S(1)} %fusion.24), channel_id=1, replica_groups=mesh['gal'=8,'pix'=32] {'pix'}, use_global_device_ids=true, to_apply=%region_5.0 | all-reduce | flops 4096 | bytes 32768 | tf_op jit(solution)/shard_map/psum | solution.py:34
  526.8 5.8 cholesky.96
  533.9 4.9 custom-call.12
  539.3 3.7 fusion.25
  543.0 146.0 %all-reduce.5.cloned.1.call-done = f32[64,512]{1,0:T(8,128)} async-done(((f32[64,512]{1,0:T(8,128)}), f32[64,512]{1,0:T(8,128)}) %all-reduce.5.cloned.1.call-update) | async-done | bytes 131088 | tf_op jit(solution)/shard_map/psum | solution.py:37
  689.0 1.2 fusion.26
  690.3 23.6 %psum.47 = f32[64,64]{0,1:T(8,128)S(1)} all-reduce(f32[64,64]{0,1:T(8,128)S(1)} %fusion.26), channel_id=1, replica_groups=mesh['gal'=8,'pix'=32] {'gal'}, use_global_device_ids=true, to_apply=%region_7.11 | all-reduce | flops 4096 | bytes 32768 | tf_op jit(solution)/shard_map/psum | solution.py:41
  714.0 5.8 cholesky.107
  721.1 4.9 custom-call.13
  726.1 8.2 %multiply_add_fusion = (f32[1024,512]{1,0:T(8,128)}, f32[1024,512]{1,0:T(8,128)}) fusion(f32[1024,512]{1,0:T(8,128)S(1)} %copy-done.1, f32[1024,512]{1,0:T(8,128)} %get-tuple-element.10, f32[1024,512]{1,0:T(8,128)} %param.9, f32[64,1024]{1,0:T(8,128)S(1)} %fusion.7, f32[64,512]{1,0:T(8,128)} %all-reduce.5.cloned.1.call-done), kind=kOutput, calls=%fused_computation | convolution fusion | flops 413663232 | bytes 10878976 | tf_op jit(solution)/shard_map/dot_general | solution.py:38
  734.3 1.0 fusion.4
  (50 shorter events, 8.2 us)
Async XLA Ops:
  7.2 0.9 copy-start
  7.2 325.0 %all-reduce.3.cloned.1.call-start = ((), (), s32[]{:S(2)}) async-start(), calls=%async_computation | async-start | bytes 262144 | tf_op jit(solution)/shard_map/psum | solution.py:37
  13.3 165.8 %copy-start.1 = (f32[1024,512]{1,0:T(8,128)S(1)}, f32[1024,512]{1,0:T(8,128)}, u32[]{:S(2)}) copy-start(f32[1024,512]{1,0:T(8,128)} %param.11) | copy-start | bytes 6291460
  13.3 1.6 collective-permute-start
  14.9 8.4 %collective-permute-start.1 = (f32[64,1024]{1,0:T(8,128)S(1)}, f32[64,1024]{1,0:T(8,128)S(1)}, u32[]{:S(2)}, u32[]{:S(2)}) collective-permute-start(f32[64,1024]{1,0:T(8,128)S(1)} %add.62), channel_id=1, source_target_pairs={{0,64},{32,96},{64,0},{96,32},{128,192},{160,224},{192,128},{224,1... | collective-permute-start | bytes 786440 | tf_op jit(solution)/shard_map/ppermute | solution.py:33
  23.4 9.1 %collective-permute-start.2 = (f32[64,1024]{1,0:T(8,128)S(1)}, f32[64,1024]{1,0:T(8,128)S(1)}, u32[]{:S(2)}, u32[]{:S(2)}) collective-permute-start(f32[64,1024]{1,0:T(8,128)S(1)} %add.63), channel_id=1, source_target_pairs={{0,128},{32,160},{64,192},{96,224},{128,0},{160,32},{192,64},{224,... | collective-permute-start | bytes 786440 | tf_op jit(solution)/shard_map/ppermute | solution.py:33
  183.6 505.5 %all-reduce.5.cloned.1.call-start = ((), (), s32[]{:S(2)}) async-start(), calls=%async_computation.1 | async-start | bytes 262144 | tf_op jit(solution)/shard_map/psum | solution.py:37
  369.3 6.2 copy-start.4
  375.5 12.6 %copy-start.2 = (f32[1024,512]{1,0:T(8,128)}, f32[1024,512]{1,0:T(8,128)S(1)}, u32[]{:S(2)}) copy-start(f32[1024,512]{1,0:T(8,128)S(1)} %get-tuple-element.9) | copy-start | bytes 6291460
  378.0 1.6 collective-permute-start.3
  379.6 8.4 %collective-permute-start.4 = (f32[64,1024]{1,0:T(8,128)S(1)}, f32[64,1024]{1,0:T(8,128)S(1)}, u32[]{:S(2)}, u32[]{:S(2)}) collective-permute-start(f32[64,1024]{1,0:T(8,128)S(1)} %add.68), channel_id=1, source_target_pairs={{0,64},{32,96},{64,0},{96,32},{128,192},{160,224},{192,128},{224,1... | collective-permute-start | bytes 786440 | tf_op jit(solution)/shard_map/ppermute | solution.py:33
  388.1 9.1 %collective-permute-start.5 = (f32[64,1024]{1,0:T(8,128)S(1)}, f32[64,1024]{1,0:T(8,128)S(1)}, u32[]{:S(2)}, u32[]{:S(2)}) collective-permute-start(f32[64,1024]{1,0:T(8,128)S(1)} %add.69), channel_id=1, source_target_pairs={{0,128},{32,160},{64,192},{96,224},{128,0},{160,32},{192,64},{224,... | collective-permute-start | bytes 786440 | tf_op jit(solution)/shard_map/ppermute | solution.py:33
  539.3 195.0 %copy-start.3 = (f32[64,1024]{1,0:T(8,128)}, f32[64,1024]{1,0:T(8,128)S(1)}, u32[]{:S(2)}) copy-start(f32[64,1024]{1,0:T(8,128)S(1)} %fusion.7) | copy-start | bytes 786436
  726.0 8.3 %copy-start.5 = (f32[64,512]{1,0:T(8,128)S(1)}, f32[64,512]{1,0:T(8,128)}, u32[]{:S(2)}) copy-start(f32[64,512]{1,0:T(8,128)} %all-reduce.5.cloned.1.call-done) | copy-start | bytes 393220
Sparse Core Ops, SparseCore 0:
  183.7 148.4 all-reduce.2
  543.2 145.8 all-reduce.4
